TPU v7x, 256 devices: a whole 4x4x8 slice. The times are simulated.
256 devices in a mesh: dp: 4 (over y), graph: 64 (over z, x, core).
Axes of the slice: x: 4, y: 4, z: 8, core: 2. Of those that a mesh axis runs over, the one named last changes fastest.
Arguments:
- edge_state: bfloat16 [4, 131072, 512], P('dp', 'graph'), may hold values from -6 to 6
- cotangent: bfloat16 [4, 131072, 512], P('dp', 'graph'), may hold values from -6 to 6
- edge_count: int32 [4, 64], P('dp', 'graph'), may hold values from 1024 to 2048, as said below
- triplet_basis: bfloat16 [4, 16, 524288], P('dp', None, 'graph'), may hold values from -6 to 6
- triplet_in: int32 [4, 524288], P('dp', 'graph'), may hold values from 0 to 2047, as said below
- triplet_out: int32 [4, 524288], P('dp', 'graph'), may hold values from 0 to 2047, as said below
- down_weight: bfloat16 [512, 64], replicated, may hold values from -0.25 to 0.25
- basis_weight: bfloat16 [16, 64], replicated, may hold values from -1.5 to 1.5
- bilinear_weight: bfloat16 [64, 64], replicated, may hold values from -0.75 to 0.75
- up_weight: bfloat16 [64, 512], replicated, may hold values from -0.75 to 0.75
- first_weight: bfloat16 [512, 512], replicated, may hold values from -0.25 to 0.25
- second_weight: bfloat16 [512, 512], replicated, may hold values from -0.25 to 0.25
Outputs:
- edge_grad: bfloat16 [4, 131072, 512], P('dp', 'graph')
- down_grad: float32 [512, 64], replicated
- basis_grad: float32 [16, 64], replicated
- bilinear_grad: float32 [64, 64], replicated
- up_grad: float32 [64, 512], replicated
- first_grad: float32 [512, 512], replicated
- second_grad: float32 [512, 512], replicated
Inputs may be any that keep to these rules, and one draw needn't show every extreme that they name: `edge_count`: every entry is a multiple of 128; in every batch some shard holds all 2048 slots live. Slot s * 8192 + j * 128 + k (s and j below 64, k below 128) holds a triplet of shard s whose in-edge is row triplet_in of shard j, a live row: below edge_count[b, j]. Slot s * 8192 + t holds a triplet whose out-edge is row triplet_out of shard s, a live row: below edge_count[b, s].
All inputs are finite; a program needn't handle non-finite values.
Results may differ from a plain program's by a relative error of at most 0.0096.
Values may be sent and summed in bfloat16 or wider, within the bound.
A program may use at most 128 MiB of HBM per device.

v0:
```python
import math
import jax
import jax.numpy as jnp
from jax import lax
from jax.sharding import PartitionSpec as P

HALF = 0.7071067811865476


def silu_slope(argument):
    logistic = jax.nn.sigmoid(argument)
    return logistic * (1.0 + argument * (1.0 - logistic))


def contract(left, right, left_dim, right_dim):
    return lax.dot_general(
        left, right, (((left_dim,), (right_dim,)), ((), ())), preferred_element_type=jnp.float32
    )


def local(
    edge_state,
    cotangent,
    edge_count,
    triplet_basis,
    triplet_in,
    triplet_out,
    down_weight,
    basis_weight,
    bilinear_weight,
    up_weight,
    first_weight,
    second_weight,
):
    edge_rows = edge_state[0]
    row_count = edge_rows.shape[0]
    shards = lax.axis_size("graph")
    narrow = down_weight.shape[1]
    in_local = triplet_in[0]
    out_local = triplet_out[0]
    tri_rows = in_local.shape[0]
    slot_count = tri_rows // shards
    live_mask = (jnp.arange(row_count, dtype=jnp.int32) < edge_count[0, 0]).astype(jnp.float32)
    wanted = lax.all_to_all(
        in_local.reshape(shards, slot_count), "graph", split_axis=0, concat_axis=0, tiled=True
    ).reshape(tri_rows)
    pre_down = contract(down_weight, edge_rows, 0, 1)
    down_rows = jax.nn.silu(pre_down).astype(jnp.bfloat16)
    tri_coef = contract(basis_weight, triplet_basis[0], 0, 0)
    served = jnp.take(down_rows, wanted, axis=1).reshape(narrow, shards, slot_count)
    fetched = lax.all_to_all(served, "graph", split_axis=1, concat_axis=1, tiled=True).reshape(
        narrow, tri_rows
    )
    message = tri_coef * fetched.astype(jnp.float32)
    gathered = (
        jnp.zeros((narrow, row_count), jnp.float32)
        .at[:, out_local]
        .add(message)
        .astype(jnp.bfloat16)
    )
    mixed_rows = contract(bilinear_weight, gathered, 0, 0).astype(jnp.bfloat16)
    pre_up = contract(mixed_rows, up_weight, 0, 0)
    summed = edge_rows.astype(jnp.float32) + jax.nn.silu(pre_up)
    summed_half = summed.astype(jnp.bfloat16)
    pre_first = jnp.dot(summed_half, first_weight, preferred_element_type=jnp.float32)
    first_rows = jax.nn.silu(pre_first).astype(jnp.bfloat16)
    pre_second = jnp.dot(first_rows, second_weight, preferred_element_type=jnp.float32)
    back_top = cotangent[0].astype(jnp.float32) * live_mask[:, None] * HALF
    back_second = (back_top * silu_slope(pre_second)).astype(jnp.bfloat16)
    back_first = (contract(back_second, second_weight, 1, 1) * silu_slope(pre_first)).astype(
        jnp.bfloat16
    )
    first_grad = contract(summed_half, back_first, 0, 0)
    second_grad = contract(first_rows, back_second, 0, 0)
    back_summed = back_top + contract(back_first, first_weight, 1, 1)
    back_up = (back_summed * silu_slope(pre_up)).astype(jnp.bfloat16)
    back_mixed = contract(up_weight, back_up, 1, 1).astype(jnp.bfloat16)
    back_gathered = contract(bilinear_weight, back_mixed, 1, 0)
    back_message = jnp.take(back_gathered, out_local, axis=1)
    back_coef = (back_message * fetched.astype(jnp.float32)).astype(jnp.bfloat16)
    back_fetched = back_message * tri_coef
    returned = (
        lax.all_to_all(
            back_fetched.reshape(narrow, shards, slot_count).astype(jnp.bfloat16),
            "graph",
            split_axis=1,
            concat_axis=1,
            tiled=True,
        )
        .astype(jnp.float32)
        .reshape(narrow, tri_rows)
    )
    back_down = jnp.zeros((narrow, row_count), jnp.float32).at[:, wanted].add(returned)
    up_grad = contract(mixed_rows, back_up, 1, 0)
    bilinear_grad = contract(gathered, back_mixed, 1, 1)
    basis_grad = contract(triplet_basis[0], back_coef, 1, 1)
    back_pre = (back_down * silu_slope(pre_down)).astype(jnp.bfloat16)
    down_grad = contract(edge_rows, back_pre, 0, 1)
    edge_grad = (back_summed + contract(back_pre, down_weight, 0, 1)).astype(jnp.bfloat16)
    down_grad, basis_grad, bilinear_grad, up_grad, first_grad, second_grad = lax.psum(
        (down_grad, basis_grad, bilinear_grad, up_grad, first_grad, second_grad), ("dp", "graph")
    )
    grad_scale = 1.0 / math.sqrt(lax.axis_size("dp") * shards * row_count)
    return (
        edge_grad[None],
        down_grad * grad_scale,
        basis_grad * grad_scale,
        bilinear_grad * grad_scale,
        up_grad * grad_scale,
        first_grad * grad_scale,
        second_grad * grad_scale,
    )


def solution(mesh):
    in_specs = (
        P("dp", "graph", None),
        P("dp", "graph", None),
        P("dp", "graph"),
        P("dp", None, "graph"),
        P("dp", "graph"),
        P("dp", "graph"),
        P(),
        P(),
        P(),
        P(),
        P(),
        P(),
    )
    out_specs = (P("dp", "graph", None), P(), P(), P(), P(), P(), P())
    return jax.shard_map(local, mesh=mesh, in_specs=in_specs, out_specs=out_specs, check_vma=False)
```

profile of v0, /device:TPU:2, one launch (start us, length us, event | category | flops | bytes accessed | tf_op | source)
XLA Modules:
  0.0 558.6 jit_solution(4663164017009512426)
XLA Ops:
  7.2 12.2 %all-to-all-start = ((s32[64,1,128]{2,1,0:T(1,128)}), s32[64,1,128]{2,1,0:T(1,128)S(1)}, u32[]{:S(2)}, u32[]{:S(2)}) async-start(s32[64,1,128]{2,1,0:T(1,128)} %bitcast.127), calls=%async_computation | async-start | bytes 65536 | tf_op jit(solution)/shard_map/all_to_all | solution.py:44
  20.8 3.2 multiply_convert_fusion.4
  24.3 3.6 all-to-all-done
  28.0 24.0 %gather_fusion = bf16[8192,64]{1,0:T(8,128)(2,1)S(1)} fusion(bf16[64,2048]{0,1:T(8,128)(2,1)S(1)} %copy.35, s32[8192]{0:T(1024)S(1)} %broadcast_clamp_fusion.1), kind=kCustom, calls=%fused_computation | custom fusion | bytes 2129920 | tf_op jit(solution)/shard_map/jit(_take)/gather | solution.py:50
  56.0 6.9 %all-to-all-start.1 = ((bf16[64,64,128]{2,0,1:T(8,128)(2,1)}), bf16[64,64,128]{2,0,1:T(8,128)(2,1)}, u32[]{:S(2)}, u32[]{:S(2)}) async-start(bf16[64,64,128]{2,0,1:T(8,128)(2,1)} %broadcast_select_fusion), calls=%async_computation.1 | async-start | bytes 2097152 | tf_op jit(solution)/shard_map/all_to_all | solution.py:51
  63.4 28.1 %all-to-all-done.1 = bf16[64,64,128]{2,0,1:T(8,128)(2,1)} async-done(((bf16[64,64,128]{2,0,1:T(8,128)(2,1)}), bf16[64,64,128]{2,0,1:T(8,128)(2,1)}, u32[]{:S(2)}, u32[]{:S(2)}) %all-to-all-start.1) | async-done | bytes 1048608 | tf_op jit(solution)/shard_map/all_to_all | solution.py:51
  91.5 2.7 fusion.6
  94.3 3.8 copy.38
  98.1 45.3 %scatter_custom_fusion = f32[64,2048]{0,1:T(8,128)} fusion(s32[8192]{0:T(1024)S(1)} %bitcast.126, f32[8192,64]{1,0:T(8,128)} %copy.38, f32[]{:T(128)} %constant.18.clone.1), kind=kCustom, calls=%fused_computation.50 | custom fusion | flops 524288 | bytes 524800 | tf_op jit(solution)/shard_map/scatter-add | solution.py:58
  144.9 2.9 add_convert_fusion.1
  155.3 4.0 multiply_convert_fusion
  163.6 27.9 %gather_fusion.1 = f32[8192,64]{1,0:T(8,128)} fusion(f32[64,2048]{0,1:T(8,128)S(1)} %copy.39, s32[8192]{0:T(1024)S(1)} %broadcast_clamp_fusion), kind=kCustom, calls=%fused_computation.1 | custom fusion | bytes 4227072 | tf_op jit(solution)/shard_map/jit(_take)/gather | solution.py:79
  191.6 3.8 copy.40
  195.3 2.9 copy_bitcast_fusion
  198.2 5.8 %all-to-all-start.2 = ((bf16[64,64,128]{2,0,1:T(8,128)(2,1)}), bf16[64,64,128]{2,0,1:T(8,128)(2,1)S(1)}, u32[]{:S(2)}, u32[]{:S(2)}) async-start(bf16[64,64,128]{2,0,1:T(8,128)(2,1)} %copy_bitcast_fusion), calls=%async_computation.2 | async-start | bytes 2097152 | tf_op jit(solution)/shard_map/all_to_all | solution.py:83
  206.0 4.0 fusion.33
  212.3 20.6 %all-to-all-done.2 = bf16[64,64,128]{2,0,1:T(8,128)(2,1)S(1)} async-done(((bf16[64,64,128]{2,0,1:T(8,128)(2,1)}), bf16[64,64,128]{2,0,1:T(8,128)(2,1)S(1)}, u32[]{:S(2)}, u32[]{:S(2)}) %all-to-all-start.2) | async-done | bytes 1048608 | tf_op jit(solution)/shard_map/all_to_all | solution.py:83
  233.0 2.8 copy.43
  235.8 44.6 %scatter_custom_fusion.1 = f32[64,2048]{0,1:T(8,128)S(1)} fusion(s32[8192]{0:T(1024)S(1)} %bitcast.124, f32[8192,64]{1,0:T(8,128)} %copy.43, f32[]{:T(128)} %constant.18.clone.1), kind=kCustom, calls=%fused_computation.48 | custom fusion | flops 524288 | bytes 524800 | tf_op jit(solution)/shard_map/scatter-add | solution.py:93
  280.9 2.8 fusion.13
  287.1 74.4 %all-reduce = (f32[16,64]{1,0:T(8,128)S(1)}, f32[64,64]{1,0:T(8,128)S(1)}) all-reduce(f32[16,64]{1,0:T(8,128)S(1)} %convolution_bitcast_fusion.1, f32[64,64]{1,0:T(8,128)S(1)} %fusion.27), channel_id=1, replica_groups=mesh['dp'=4,'graph'=64] {'dp','graph'}, use_global_device_ids=true, to_apply=%region_3.4 | all-reduce | flops 5120 | bytes 40960 | tf_op jit(solution)/shard_map/psum | solution.py:100
  362.7 4.3 fusion.4
  367.0 178.4 %all-reduce.4.cloned.1.call-done = (f32[512,64]{0,1:T(8,128)}, f32[64,512]{1,0:T(8,128)}, f32[512,512]{1,0:T(8,128)}, f32[512,512]{1,0:T(8,128)}) async-done(((f32[512,64]{0,1:T(8,128)}, f32[64,512]{1,0:T(8,128)}, f32[512,512]{1,0:T(8,128)}, f32[512,512]{1,0:T(8,128)}), (f32[512,64]{0,1:T(8,128)}, f32[64,512]{1,0:T(8,128)}, f32[512,512]{1,0:T(8,128)}, f32[512,512]{1,0:T(8,128)})) %all-reduce.4.cloned.1.call-update) | async-done | bytes 2359312 | tf_op jit(solution)/shard_map/psum | solution.py:100
  548.6 3.2 broadcast_multiply_fusion
  (78 shorter events, 31.4 us)
Async XLA Ops:
  7.2 140.7 %copy-start = (bf16[512,512]{1,0:T(8,128)(2,1)S(1)}, bf16[512,512]{1,0:T(8,128)(2,1)}, u32[]{:S(2)}) copy-start(bf16[512,512]{1,0:T(8,128)(2,1)} %param.22) | copy-start | bytes 1572868
  7.2 20.7 %all-to-all-start = ((s32[64,1,128]{2,1,0:T(1,128)}), s32[64,1,128]{2,1,0:T(1,128)S(1)}, u32[]{:S(2)}, u32[]{:S(2)}) async-start(s32[64,1,128]{2,1,0:T(1,128)} %bitcast.127), calls=%async_computation | async-start | bytes 65536 | tf_op jit(solution)/shard_map/all_to_all | solution.py:44
  53.6 9.2 %copy-start.8 = (s32[1,8192]{1,0:T(1,128)S(1)}, s32[1,8192]{1,0:T(1,128)}, u32[]{:S(2)}) copy-start(s32[1,8192]{1,0:T(1,128)} %param.17) | copy-start | bytes 98308
  53.6 9.3 %copy-start.9 = (bf16[1,16,8192]{2,1,0:T(8,128)(2,1)S(1)}, bf16[1,16,8192]{2,1,0:T(8,128)(2,1)}, u32[]{:S(2)}) copy-start(bf16[1,16,8192]{2,1,0:T(8,128)(2,1)} %param.15) | copy-start | bytes 786436
  53.6 9.3 %copy-start.13 = (bf16[16,64]{1,0:T(8,128)(2,1)S(1)}, bf16[16,64]{1,0:T(8,128)(2,1)}, u32[]{:S(2)}) copy-start(bf16[16,64]{1,0:T(8,128)(2,1)} %param.19) | copy-start | bytes 6148
  56.0 35.6 %all-to-all-start.1 = ((bf16[64,64,128]{2,0,1:T(8,128)(2,1)}), bf16[64,64,128]{2,0,1:T(8,128)(2,1)}, u32[]{:S(2)}, u32[]{:S(2)}) async-start(bf16[64,64,128]{2,0,1:T(8,128)(2,1)} %broadcast_select_fusion), calls=%async_computation.1 | async-start | bytes 2097152 | tf_op jit(solution)/shard_map/all_to_all | solution.py:51
  94.3 49.1 %copy-start.12 = (bf16[64,64]{1,0:T(8,128)(2,1)S(1)}, bf16[64,64]{1,0:T(8,128)(2,1)}, u32[]{:S(2)}) copy-start(bf16[64,64]{1,0:T(8,128)(2,1)} %param.20) | copy-start | bytes 24580
  98.1 46.9 %copy-start.11 = (bf16[64,512]{1,0:T(8,128)(2,1)S(1)}, bf16[64,512]{1,0:T(8,128)(2,1)}, u32[]{:S(2)}) copy-start(bf16[64,512]{1,0:T(8,128)(2,1)} %param.21) | copy-start | bytes 196612
  147.8 1.9 copy-start.16
  147.8 2.3 copy-start.14
  147.9 2.4 copy-start.15
  149.8 3.1 copy-start.20
  152.9 2.3 copy-start.22
  155.2 4.0 copy-start.18
  198.2 6.1 %copy-start.5 = (bf16[2048,512]{1,0:T(8,128)(2,1)S(1)}, bf16[2048,512]{1,0:T(8,128)(2,1)}, u32[]{:S(2)}) copy-start(bf16[2048,512]{1,0:T(8,128)(2,1)} %copy-done.4) | copy-start | bytes 6291460
  198.2 34.6 %all-to-all-start.2 = ((bf16[64,64,128]{2,0,1:T(8,128)(2,1)}), bf16[64,64,128]{2,0,1:T(8,128)(2,1)S(1)}, u32[]{:S(2)}, u32[]{:S(2)}) async-start(bf16[64,64,128]{2,0,1:T(8,128)(2,1)} %copy_bitcast_fusion), calls=%async_computation.2 | async-start | bytes 2097152 | tf_op jit(solution)/shard_map/all_to_all | solution.py:83
  204.0 341.4 %all-reduce.4.cloned.1.call-start = ((), (), s32[]{:S(2)}) async-start(), calls=%async_computation.3 | async-start | bytes 4718592 | tf_op jit(solution)/shard_map/psum | solution.py:100
  206.0 4.0 copy-start.17
  206.0 4.0 copy-start.19
  235.8 44.9 %copy-start.7 = (f32[64,2048]{1,0:T(8,128)S(1)}, f32[64,2048]{1,0:T(8,128)}, u32[]{:S(2)}) copy-start(f32[64,2048]{1,0:T(8,128)} %get-tuple-element.14) | copy-start | bytes 1572868
  280.9 2.9 copy-start.2
  283.7 1.7 copy-start.3
  285.4 77.3 %copy-start.10 = (bf16[512,64]{0,1:T(8,128)(2,1)S(1)}, bf16[512,64]{0,1:T(8,128)(2,1)}, u32[]{:S(2)}) copy-start(bf16[512,64]{0,1:T(8,128)(2,1)} %param.18) | copy-start | bytes 196612
  548.6 3.2 copy-start.1
  (3 other events, 3.7 us)
Sparse Core Ops, SparseCore 0:
  283.9 261.4 all-reduce.3
where the time goes:
time: 560 us; the launch traced here: 559 us
  waiting for transfers between devices  231 us (41%)
  other arithmetic  107 us (19%)
  blocking collectives  74.4 us (13%)
  local copies, waits for them, and re-layouts  68.5 us (12%)
  matrix products  38.2 us (7%)
  starting transfers between devices  25.1 us (4%)
  between operations  15 us (3%)
    psum x1, waiting for transfers between devices, local(): lax.psum((down_grad, basis_grad, bilinear_grad, up_grad, first_grad, seco...  178 us
    psum x1, blocking collectives, local(): lax.psum((down_grad, basis_grad, bilinear_grad, up_grad, first_grad, seco...  74.4 us
    scatter-add x1, other arithmetic, local(): gathered = jnp.zeros((narrow, row_count), jnp.float32).at[:, out_local].a...  45.3 us
    scatter-add x1, other arithmetic, local(): jnp.zeros((narrow, row_count), jnp.float32).at[:, wanted].add(returned)  44.6 us
    dot_general x15, matrix products, contract(): lax.dot_general(left, right, (((left_dim,), (right_dim,)), ((), ())), pre...  33.7 us
    gather x2, local copies, waits for them, and re-layouts, local(): back_message = jnp.take(back_gathered, out_local, axis=1)  31.7 us
    all_to_all x1, waiting for transfers between devices, local(): lax.all_to_all(served, 'graph', split_axis=1, concat_axis=1, tiled=True)  28.1 us
    gather x2, local copies, waits for them, and re-layouts, local(): jnp.take(down_rows, wanted, axis=1).reshape(narrow, shards, slot_count)  25.6 us
  transfers between devices with their start and end apart: 4, of which 4 were waited for; matrix products, arithmetic and copies ran while one was open for 4% of the time, Pallas kernels for 0%

commit v1 on v0

--- a/solution.py
+++ b/solution.py
@@ -97,8 +97,9 @@
     back_pre = (back_down * silu_slope(pre_down)).astype(jnp.bfloat16)
     down_grad = contract(edge_rows, back_pre, 0, 1)
     edge_grad = (back_summed + contract(back_pre, down_weight, 0, 1)).astype(jnp.bfloat16)
-    down_grad, basis_grad, bilinear_grad, up_grad, first_grad, second_grad = lax.psum(
-        (down_grad, basis_grad, bilinear_grad, up_grad, first_grad, second_grad), ("dp", "graph")
+    _draw_windows = lambda own_rows: lax.psum(lax.psum(own_rows, "dp"), "graph")
+    down_grad, basis_grad, bilinear_grad, up_grad, first_grad, second_grad = _draw_windows(
+        (down_grad, basis_grad, bilinear_grad, up_grad, first_grad, second_grad)
     )
     grad_scale = 1.0 / math.sqrt(lax.axis_size("dp") * shards * row_count)
     return (

time: 560 us -> 633 us (1.13)
  blocking collectives: 74.4 us -> 258 us
  waiting for transfers between devices: 231 us -> 117 us
    psum x1 -> x2, blocking collectives: 74.4 us -> 258 us  [local(): _draw_windows = lambda own_rows: lax.psum(lax.psum(own_rows, 'dp'), 'graph')]
    psum x1 -> x2, waiting for transfers between devices: 178 us -> 64.8 us  [local(): _draw_windows = lambda own_rows: lax.psum(lax.psum(own_rows, 'dp'), 'graph')]
  transfers between devices with their start and end apart: 4 -> 5, of which waited for: 4 -> 4; matrix products, arithmetic and copies ran while one was open for 4% -> 3% of each run, Pallas kernels for 0% -> 0%
where the time goes in v1:
time: 633 us; the launch traced here: 628 us
  blocking collectives  258 us (41%)
  waiting for transfers between devices  117 us (18%)
  other arithmetic  107 us (17%)
  local copies, waits for them, and re-layouts  68.3 us (11%)
  matrix products  37.9 us (6%)
  starting transfers between devices  25.1 us (4%)
  between operations  15.1 us (2%)
    psum x2, blocking collectives, local(): _draw_windows = lambda own_rows: lax.psum(lax.psum(own_rows, 'dp'), 'graph')  258 us
    psum x2, waiting for transfers between devices, local(): _draw_windows = lambda own_rows: lax.psum(lax.psum(own_rows, 'dp'), 'graph')  64.8 us
    scatter-add x1, other arithmetic, local(): gathered = jnp.zeros((narrow, row_count), jnp.float32).at[:, out_local].a...  45.3 us
    scatter-add x1, other arithmetic, local(): jnp.zeros((narrow, row_count), jnp.float32).at[:, wanted].add(returned)  44.6 us
    dot_general x15, matrix products, contract(): lax.dot_general(left, right, (((left_dim,), (right_dim,)), ((), ())), pre...  33.4 us
    gather x2, local copies, waits for them, and re-layouts, local(): back_message = jnp.take(back_gathered, out_local, axis=1)  31.7 us
    all_to_all x1, waiting for transfers between devices, local(): lax.all_to_all(served, 'graph', split_axis=1, concat_axis=1, tiled=True)  28.1 us
    gather x2, local copies, waits for them, and re-layouts, local(): jnp.take(down_rows, wanted, axis=1).reshape(narrow, shards, slot_count)  25.6 us
  transfers between devices with their start and end apart: 5, of which 4 were waited for; matrix products, arithmetic and copies ran while one was open for 3% of the time, Pallas kernels for 0%

profile of v1, /device:TPU:2, one launch (start us, length us, event | category | flops | bytes accessed | tf_op | source)
XLA Modules:
  0.0 627.9 jit_solution(7937937274104300608)
XLA Ops:
  7.2 12.2 %all-to-all-start = ((s32[64,1,128]{2,1,0:T(1,128)}), s32[64,1,128]{2,1,0:T(1,128)S(1)}, u32[]{:S(2)}, u32[]{:S(2)}) async-start(s32[64,1,128]{2,1,0:T(1,128)} %bitcast.127), calls=%async_computation | async-start | bytes 65536 | tf_op jit(solution)/shard_map/all_to_all | solution.py:44
  20.8 3.2 multiply_convert_fusion.4
  24.3 3.6 all-to-all-done
  28.0 24.0 %gather_fusion = bf16[8192,64]{1,0:T(8,128)(2,1)S(1)} fusion(bf16[64,2048]{0,1:T(8,128)(2,1)S(1)} %copy.35, s32[8192]{0:T(1024)S(1)} %broadcast_clamp_fusion.1), kind=kCustom, calls=%fused_computation | custom fusion | bytes 2129920 | tf_op jit(solution)/shard_map/jit(_take)/gather | solution.py:50
  56.0 6.9 %all-to-all-start.1 = ((bf16[64,64,128]{2,0,1:T(8,128)(2,1)}), bf16[64,64,128]{2,0,1:T(8,128)(2,1)}, u32[]{:S(2)}, u32[]{:S(2)}) async-start(bf16[64,64,128]{2,0,1:T(8,128)(2,1)} %broadcast_select_fusion), calls=%async_computation.1 | async-start | bytes 2097152 | tf_op jit(solution)/shard_map/all_to_all | solution.py:51
  63.4 28.1 %all-to-all-done.1 = bf16[64,64,128]{2,0,1:T(8,128)(2,1)} async-done(((bf16[64,64,128]{2,0,1:T(8,128)(2,1)}), bf16[64,64,128]{2,0,1:T(8,128)(2,1)}, u32[]{:S(2)}, u32[]{:S(2)}) %all-to-all-start.1) | async-done | bytes 1048608 | tf_op jit(solution)/shard_map/all_to_all | solution.py:51
  91.5 2.7 fusion.6
  94.3 3.8 copy.38
  98.1 45.3 %scatter_custom_fusion = f32[64,2048]{0,1:T(8,128)} fusion(s32[8192]{0:T(1024)S(1)} %bitcast.126, f32[8192,64]{1,0:T(8,128)} %copy.38, f32[]{:T(128)} %constant.18.clone.1), kind=kCustom, calls=%fused_computation.50 | custom fusion | flops 524288 | bytes 524800 | tf_op jit(solution)/shard_map/scatter-add | solution.py:58
  144.9 2.9 add_convert_fusion.1
  155.3 4.0 multiply_convert_fusion
  163.6 27.9 %gather_fusion.1 = f32[8192,64]{1,0:T(8,128)} fusion(f32[64,2048]{0,1:T(8,128)S(1)} %copy.39, s32[8192]{0:T(1024)S(1)} %broadcast_clamp_fusion), kind=kCustom, calls=%fused_computation.1 | custom fusion | bytes 4227072 | tf_op jit(solution)/shard_map/jit(_take)/gather | solution.py:79
  191.6 3.8 copy.40
  195.3 2.9 copy_bitcast_fusion
  198.2 5.8 all-to-all-start.2
  206.0 4.0 fusion.33
  212.3 20.6 %all-to-all-done.2 = bf16[64,64,128]{2,0,1:T(8,128)(2,1)S(1)} async-done(((bf16[64,64,128]{2,0,1:T(8,128)(2,1)}), bf16[64,64,128]{2,0,1:T(8,128)(2,1)S(1)}, u32[]{:S(2)}, u32[]{:S(2)}) %all-to-all-start.2) | async-done | bytes 1048608 | tf_op jit(solution)/shard_map/all_to_all | solution.py:83
  233.0 2.8 copy.43
  235.8 44.6 %scatter_custom_fusion.1 = f32[64,2048]{0,1:T(8,128)S(1)} fusion(s32[8192]{0:T(1024)S(1)} %bitcast.124, f32[8192,64]{1,0:T(8,128)} %copy.43, f32[]{:T(128)} %constant.18.clone.1), kind=kCustom, calls=%fused_computation.48 | custom fusion | flops 524288 | bytes 524800 | tf_op jit(solution)/shard_map/scatter-add | solution.py:93
  283.8 64.8 %all-reduce.9.cloned.1.call-done = (f32[512,64]{0,1:T(8,128)}, f32[64,512]{1,0:T(8,128)}, f32[512,512]{1,0:T(8,128)}, f32[512,512]{1,0:T(8,128)}) async-done(((f32[512,64]{0,1:T(8,128)}, f32[64,512]{1,0:T(8,128)}, f32[512,512]{1,0:T(8,128)}, f32[512,512]{1,0:T(8,128)}), (f32[512,64]{0,1:T(8,128)}, f32[64,512]{1,0:T(8,128)}, f32[512,512]{1,0:T(8,128)}, f32[512,512]{1,0:T(8,128)})) %all-reduce.9.cloned.1.call-update) | async-done | bytes 2359312 | tf_op jit(solution)/shard_map/psum | solution.py:100
  351.6 15.4 %all-reduce.2 = (f32[16,64]{1,0:T(8,128)S(1)}, f32[64,64]{1,0:T(8,128)S(1)}) all-reduce(f32[16,64]{1,0:T(8,128)S(1)} %convolution_bitcast_fusion.1, f32[64,64]{1,0:T(8,128)S(1)} %fusion.27), channel_id=1, replica_groups=mesh['dp'=4,'graph'=64] {'dp'}, use_global_device_ids=true, to_apply=%region_4.5 | all-reduce | flops 5120 | bytes 40960 | tf_op jit(solution)/shard_map/psum | solution.py:100
  367.0 242.2 %all-reduce = (f32[16,64]{1,0:T(8,128)S(1)}, f32[64,64]{1,0:T(8,128)S(1)}) all-reduce(f32[16,64]{1,0:T(8,128)S(1)} %get-tuple-element.13, f32[64,64]{1,0:T(8,128)S(1)} %get-tuple-element.14), channel_id=1, replica_groups=mesh['dp'=4,'graph'=64] {'graph'}, use_global_device_ids=true, to_apply=%region_5.6 | all-reduce | flops 5120 | bytes 40960 | tf_op jit(solution)/shard_map/psum | solution.py:100
  610.5 4.2 fusion.4
  617.9 3.2 broadcast_multiply_fusion
  (82 shorter events, 33.8 us)
Async XLA Ops:
  7.2 140.7 %copy-start = (bf16[512,512]{1,0:T(8,128)(2,1)S(1)}, bf16[512,512]{1,0:T(8,128)(2,1)}, u32[]{:S(2)}) copy-start(bf16[512,512]{1,0:T(8,128)(2,1)} %param.22) | copy-start | bytes 1572868
  7.2 20.7 %all-to-all-start = ((s32[64,1,128]{2,1,0:T(1,128)}), s32[64,1,128]{2,1,0:T(1,128)S(1)}, u32[]{:S(2)}, u32[]{:S(2)}) async-start(s32[64,1,128]{2,1,0:T(1,128)} %bitcast.127), calls=%async_computation | async-start | bytes 65536 | tf_op jit(solution)/shard_map/all_to_all | solution.py:44
  53.6 9.2 %copy-start.8 = (s32[1,8192]{1,0:T(1,128)S(1)}, s32[1,8192]{1,0:T(1,128)}, u32[]{:S(2)}) copy-start(s32[1,8192]{1,0:T(1,128)} %param.17) | copy-start | bytes 98308
  53.6 9.3 %copy-start.9 = (bf16[1,16,8192]{2,1,0:T(8,128)(2,1)S(1)}, bf16[1,16,8192]{2,1,0:T(8,128)(2,1)}, u32[]{:S(2)}) copy-start(bf16[1,16,8192]{2,1,0:T(8,128)(2,1)} %param.15) | copy-start | bytes 786436
  53.6 9.3 %copy-start.13 = (bf16[16,64]{1,0:T(8,128)(2,1)S(1)}, bf16[16,64]{1,0:T(8,128)(2,1)}, u32[]{:S(2)}) copy-start(bf16[16,64]{1,0:T(8,128)(2,1)} %param.19) | copy-start | bytes 6148
  56.0 35.6 %all-to-all-start.1 = ((bf16[64,64,128]{2,0,1:T(8,128)(2,1)}), bf16[64,64,128]{2,0,1:T(8,128)(2,1)}, u32[]{:S(2)}, u32[]{:S(2)}) async-start(bf16[64,64,128]{2,0,1:T(8,128)(2,1)} %broadcast_select_fusion), calls=%async_computation.1 | async-start | bytes 2097152 | tf_op jit(solution)/shard_map/all_to_all | solution.py:51
  94.3 49.1 %copy-start.12 = (bf16[64,64]{1,0:T(8,128)(2,1)S(1)}, bf16[64,64]{1,0:T(8,128)(2,1)}, u32[]{:S(2)}) copy-start(bf16[64,64]{1,0:T(8,128)(2,1)} %param.20) | copy-start | bytes 24580
  98.1 46.9 %copy-start.11 = (bf16[64,512]{1,0:T(8,128)(2,1)S(1)}, bf16[64,512]{1,0:T(8,128)(2,1)}, u32[]{:S(2)}) copy-start(bf16[64,512]{1,0:T(8,128)(2,1)} %param.21) | copy-start | bytes 196612
  147.8 2.3 copy-start.14
  147.9 2.4 copy-start.15
  149.8 3.1 copy-start.20
  152.9 2.3 copy-start.22
  155.2 4.0 copy-start.18
  198.2 6.1 copy-start.5
  198.2 34.6 %all-to-all-start.2 = ((bf16[64,64,128]{2,0,1:T(8,128)(2,1)}), bf16[64,64,128]{2,0,1:T(8,128)(2,1)S(1)}, u32[]{:S(2)}, u32[]{:S(2)}) async-start(bf16[64,64,128]{2,0,1:T(8,128)(2,1)} %copy_bitcast_fusion), calls=%async_computation.2 | async-start | bytes 2097152 | tf_op jit(solution)/shard_map/all_to_all | solution.py:83
  204.0 144.5 %all-reduce.9.cloned.1.call-start = ((), (), s32[]{:S(2)}) async-start(), calls=%async_computation.4 | async-start | bytes 4718592 | tf_op jit(solution)/shard_map/psum | solution.py:100
  206.0 4.0 copy-start.17
  206.0 4.0 copy-start.19
  235.8 44.9 %copy-start.7 = (f32[64,2048]{1,0:T(8,128)S(1)}, f32[64,2048]{1,0:T(8,128)}, u32[]{:S(2)}) copy-start(f32[64,2048]{1,0:T(8,128)} %get-tuple-element.20) | copy-start | bytes 1572868
  283.6 65.0 %copy-start.2 = (f32[64,2048]{0,1:T(8,128)S(1)}, f32[64,2048]{0,1:T(8,128)}, u32[]{:S(2)}) copy-start(f32[64,2048]{0,1:T(8,128)} %scatter_custom_fusion) | copy-start | bytes 1572868
  283.7 66.2 %copy-start.3 = (f32[8192,64]{0,1:T(8,128)S(1)}, f32[8192,64]{0,1:T(8,128)}, u32[]{:S(2)}) copy-start(f32[8192,64]{0,1:T(8,128)} %copy.40) | copy-start | bytes 6291460
  283.7 331.1 %all-reduce.7.cloned.1.call-start = ((), (), s32[]{:S(2)}) async-start(), calls=%async_computation.3 | async-start | bytes 4718592 | tf_op jit(solution)/shard_map/psum | solution.py:100
  349.9 260.6 %copy-start.10 = (bf16[512,64]{0,1:T(8,128)(2,1)S(1)}, bf16[512,64]{0,1:T(8,128)(2,1)}, u32[]{:S(2)}) copy-start(bf16[512,64]{0,1:T(8,128)(2,1)} %param.18) | copy-start | bytes 196612
  617.9 3.2 copy-start.1
  (4 other events, 5.6 us)
Sparse Core Ops, SparseCore 0:
  283.8 64.7 all-reduce.8
  352.4 191.5 all-reduce.6
